TPU v7x, 32 devices: a whole 2x2x4 slice. The times are simulated.
32 devices in a mesh: groups: 2 (over y), patch: 4 (over z), req: 4 (over x, core).
Axes of the slice: x: 2, y: 2, z: 4, core: 2. Of those that a mesh axis runs over, the one named last changes fastest.
Arguments:
- hidden: bfloat16 [2, 8, 2, 128, 1152], P(None, ('groups', 'req'), None, 'patch'), parts along dimension 1, may hold values from -6 to 6
- stale_kv: bfloat16 [8, 2, 128, 1152], P(('groups', 'req'), None, 'patch'), parts along dimension 0
- cond_kv: bfloat16 [8, 128, 1152], P(('groups', 'req')), parts along dimension 0
- uncond_kv: bfloat16 [128, 1152], P('req')
- text_len: int32 [8], P(('groups', 'req')), parts along dimension 0, may hold values from 1 to 128, as said below
- timestep: int32 [8, 2], P(('groups', 'req')), parts along dimension 0, may hold values from 0 to 19
- mod_table: float32 [20, 3, 1152], replicated, may hold values from -4 to 4
- w_qkv: bfloat16 [1152, 1728], P('req'), may hold values from -0.26953125 to 0.26953125
- w_out: bfloat16 [576, 1152], P('req'), may hold values from -0.25 to 0.25
- w_cq: bfloat16 [1152, 576], P('req'), may hold values from -0.26953125 to 0.26953125
- w_co: bfloat16 [576, 1152], P('req'), may hold values from -0.25 to 0.25
Outputs:
- mixed: bfloat16 [2, 8, 2, 128, 1152], P(None, ('groups', 'req'), None, 'patch'), parts along dimension 1
- next_kv: bfloat16 [8, 2, 128, 1152], P(('groups', 'req'), None, 'patch'), parts along dimension 0
There are 2 independent parts, one for each index of `groups`. A program takes and returns all parts, laid end to end along the dimension named above; an argument that names none is the same for every part. Nothing has to cross between parts.
Inputs may be any that keep to these rules, and one draw needn't show every extreme that they name: `text_len`: some request's prompt has all 128 tokens.
All inputs are finite; a program needn't handle non-finite values.
Results may differ from a plain program's by a relative error of at most 0.02.
Values may be sent and summed in bfloat16 or wider, within the bound.
A program may use at most 128 MiB of HBM per device.

v0:
```python
import math

import jax
import jax.numpy as jnp
from jax import lax
from jax.sharding import PartitionSpec as P

HEADS = 8
HDIM = 72


def layer_norm(values):
    center = values - jnp.mean(values, axis=-1, keepdims=True)
    spread = jnp.mean(center * center, axis=-1, keepdims=True)
    return center * lax.rsqrt(spread + 1e-06)


def attend(query, pairs, mask):
    batch, count, inner = query.shape
    keys_n = pairs.shape[1]
    factor = 1.0 / math.sqrt(HDIM)
    q_heads = query.reshape(batch, count, HEADS, HDIM)
    k_heads = pairs[:, :, :inner].reshape(batch, keys_n, HEADS, HDIM)
    v_heads = pairs[:, :, inner:].reshape(batch, keys_n, HEADS, HDIM)
    scores = (
        jnp.einsum("bqhd,bkhd->bhqk", q_heads, k_heads, preferred_element_type=jnp.float32) * factor
    )
    if mask is not None:
        scores = jnp.where(mask[:, None, None, :], scores, -1e30)
    peak = jnp.max(scores, axis=-1, keepdims=True)
    expo = jnp.exp(scores - peak)
    total = jnp.sum(expo, axis=-1)
    weights = expo.astype(jnp.bfloat16)
    summed = jnp.einsum("bhqk,bkhd->bqhd", weights, v_heads, preferred_element_type=jnp.float32)
    result = summed / jnp.transpose(total, (0, 2, 1))[..., None]
    return result.reshape(batch, count, inner).astype(jnp.bfloat16)


def neighbours(local):
    return lax.all_gather(local, "patch", axis=2, tiled=True)


def per_device(
    hidden, stale_kv, cond_kv, uncond_kv, text_len, timestep, mod_table, w_qkv, w_out, w_cq, w_co
):
    steps_n, req_here, pair_n, tok_here, width = hidden.shape
    inner = w_cq.shape[1]
    text_n = cond_kv.shape[1]
    onehot = (timestep[:, :, None] == jnp.arange(mod_table.shape[0], dtype=jnp.int32)).astype(
        jnp.float32
    )
    mods = jnp.einsum("rst,tcd->srcd", onehot, mod_table, precision=lax.Precision.HIGHEST)
    shift = mods[:, :, 0][:, :, None, None, :]
    scale = mods[:, :, 1][:, :, None, None, :]
    gate = mods[:, :, 2][:, :, None, None, :]
    source = hidden.astype(jnp.float32)
    modulated = (layer_norm(source) * (1.0 + scale) + shift).astype(jnp.bfloat16)
    flat = modulated.reshape(-1, width)
    qkv = jnp.dot(
        flat, lax.all_gather(w_qkv, "req", axis=0, tiled=True), preferred_element_type=jnp.float32
    )
    whole_out, whole_cq, whole_co = (
        lax.all_gather(w_out, "req", axis=0, tiled=True),
        lax.all_gather(w_cq, "req", axis=0, tiled=True),
        lax.all_gather(w_co, "req", axis=0, tiled=True),
    )
    qkv = qkv.astype(jnp.bfloat16).reshape(steps_n, req_here, pair_n, tok_here, 3 * inner)
    queries = qkv[..., :inner]
    fresh = qkv[..., inner:]
    negative = lax.all_gather(uncond_kv, "req", axis=0, tiled=True)
    negative = negative[None]
    text_mask = jnp.arange(text_n, dtype=jnp.int32)[None, :] < text_len[:, None]
    position = lax.axis_index("patch") * tok_here
    batch = req_here * pair_n
    results = []
    earlier = neighbours(stale_kv)
    later = None
    for step in range(2):
        q_step = queries[step].reshape(batch, tok_here, inner)
        pairs = lax.dynamic_update_slice_in_dim(earlier, fresh[step], position, 2)
        pairs = pairs.reshape(batch, pairs.shape[2], 2 * inner)
        attended = attend(q_step, pairs, None)
        if step == 0:
            later = neighbours(fresh[0])
            earlier = later
        projected = jnp.dot(
            attended.reshape(-1, inner), whole_out, preferred_element_type=jnp.float32
        )
        x_one = (
            source[step] + gate[step] * projected.reshape(req_here, pair_n, tok_here, width)
        ).astype(jnp.bfloat16)
        cross_query = jnp.dot(
            x_one.reshape(-1, width), whole_cq, preferred_element_type=jnp.float32
        ).astype(jnp.bfloat16)
        cross_query = cross_query.reshape(req_here, pair_n, tok_here, inner)
        cond_out = attend(cross_query[:, 0], cond_kv, text_mask)
        uncond_out = attend(cross_query[:, 1], negative, None)
        cross = jnp.stack([cond_out, uncond_out], axis=1)
        added = jnp.dot(cross.reshape(-1, inner), whole_co, preferred_element_type=jnp.float32)
        mixed = (
            x_one.astype(jnp.float32) + added.reshape(req_here, pair_n, tok_here, width)
        ).astype(jnp.bfloat16)
        results.append(mixed)
    return (jnp.stack(results, axis=0), fresh[1])


def solution(mesh):
    placed = (
        P(None, ("groups", "req"), None, "patch", None),
        P(("groups", "req"), None, "patch", None),
        P(("groups", "req"), None, None),
        P("req", None),
        P(("groups", "req")),
        P(("groups", "req"), None),
        P(),
        P("req", None),
        P("req", None),
        P("req", None),
        P("req", None),
    )
    return jax.shard_map(
        per_device,
        mesh=mesh,
        in_specs=placed,
        out_specs=(
            P(None, ("groups", "req"), None, "patch", None),
            P(("groups", "req"), None, "patch", None),
        ),
        check_vma=False,
    )
```

profile of v0, /device:TPU:0, one launch (start us, length us, event | category | flops | bytes accessed | tf_op | source)
XLA Modules:
  0.0 117.8 jit_solution(5810013402645000020)
XLA Ops:
  7.2 0.7 all-gather.6.cloned.1.call-update
  8.0 0.7 all-gather.8.cloned.1.call-update
  8.7 0.7 all-gather.10.cloned.1.call-update
  9.5 0.5 all-gather.12.cloned.1.call-update
  10.0 0.3 convolution_bitcast_fusion
  10.3 0.6 slice_reduce_fusion.1
  11.2 0.2 multiply_reduce_fusion
  11.4 18.2 %all_gather.21 = bf16[1,2,128,1152]{3,2,1,0:T(8,128)(2,1)S(1)} all-gather(bf16[1,2,32,1152]{3,2,1,0:T(8,128)(2,1)S(1)} %copy-done.16), channel_id=1, replica_groups=mesh['groups'=2,'patch'=4,'req'=4] {'patch'}, dimensions={2}, use_global_device_ids=true | all-gather | bytes 737280 | tf_op jit(solution)/shard_map/all_gather | solution.py:40
  30.5 0.8 copy.30
  31.3 7.9 %all_gather.25 = bf16[128,1152]{1,0:T(8,128)(2,1)S(1)} all-gather(bf16[32,1152]{1,0:T(8,128)(2,1)S(1)} %copy-done.17), channel_id=1, replica_groups=mesh['groups'=2,'patch'=4,'req'=4] {'req'}, dimensions={0}, use_global_device_ids=true | all-gather | bytes 368640 | tf_op jit(solution)/shard_map/all_gather | solution.py:70
  39.5 0.8 copy.34
  40.3 0.2 add_convert_fusion
  40.6 7.5 %all-gather.6.cloned.1.call-done = bf16[1152,1728]{1,0:T(8,128)(2,1)} async-done(((bf16[288,1728]{1,0:T(8,128)(2,1)}), bf16[1152,1728]{1,0:T(8,128)(2,1)}) %all-gather.6.cloned.1.call-update) | async-done | bytes 3981328 | tf_op jit(solution)/shard_map/all_gather | solution.py:60
  48.0 3.8 %convolution_convert_fusion = bf16[128,1728]{0,1:T(8,128)(2,1)S(1)} fusion(bf16[128,1152]{1,0:T(8,128)(2,1)S(1)} %bitcast.202, bf16[1152,1728]{1,0:T(8,128)(2,1)} %all-gather.6.cloned.1.call-done), kind=kOutput, calls=%fused_computation | convolution fusion | flops 509829120 | bytes 4718592 | tf_op jit(solution)/shard_map/dot_general | solution.py:59
  51.8 0.2 copy.23
  52.1 0.8 slice_bitcast_fusion.2
  52.9 0.6 fusion.69
  53.5 17.1 %all-gather = bf16[1,1,2,128,1152]{4,3,2,0,1:T(8,128)(2,1)S(1)} all-gather(bf16[1,1,2,32,1152]{4,3,2,0,1:T(8,128)(2,1)S(1)} %get-tuple-element.9), channel_id=2, replica_groups=mesh['groups'=2,'patch'=4,'req'=4] {'patch'}, dimensions={3}, use_global_device_ids=true | all-gather | bytes 737280 | tf_op jit(solution)/shard_map/all_gather | solution.py:40
  70.8 0.4 fusion.67
  71.2 0.2 copy.25
  71.4 1.0 reshape_reshape_squeeze.6
  72.7 0.3 fusion.77
  73.0 0.3 fusion.26
  73.2 0.3 fusion.14
  73.8 1.7 %fusion.2 = bf16[2,32,1152]{2,1,0:T(8,128)(2,1)S(1)} fusion(bf16[2,32,576]{2,1,0:T(8,128)(2,1)S(1)} %convert_element_type.143, bf16[576,1152]{1,0:T(8,128)(2,1)} %all-gather.8.cloned.1.call-done, f32[2,1,2,32,1152]{4,3,2,1,0:T(8,128)S(1)} %convert_element_type.138, f32[1152]{0:T(1024)S(1)} %get-tuple-element.2), kind=kOutput, calls=%fused_computation.7 | convolution fusion | flops 85155840 | bytes 1847808 | tf_op jit(solution)/shard_map/dot_general | solution.py:86
  75.5 13.1 %all-gather.10.cloned.1.call-done = bf16[1152,576]{1,0:T(8,128)(2,1)} async-done(((bf16[288,576]{1,0:T(8,128)(2,1)}), bf16[1152,576]{1,0:T(8,128)(2,1)}) %all-gather.10.cloned.1.call-update) | async-done | bytes 1327120 | tf_op jit(solution)/shard_map/all_gather | solution.py:64
  88.6 1.7 %convolution_convert_fusion.2 = bf16[64,576]{1,0:T(8,128)(2,1)S(1)} fusion(bf16[64,1152]{1,0:T(8,128)(2,1)S(1)} %bitcast.195, bf16[1152,576]{1,0:T(8,128)(2,1)} %all-gather.10.cloned.1.call-done), kind=kOutput, calls=%fused_computation.37 | convolution fusion | flops 84971520 | bytes 1548288 | tf_op jit(solution)/shard_map/dot_general | solution.py:92
  90.6 0.2 copy.37
  91.2 0.2 fusion.79
  91.7 0.3 fusion.19
  92.0 0.2 fusion.78
  92.4 0.3 fusion.74
  92.7 0.3 fusion.28
  93.0 1.0 fusion.15
  94.0 0.3 fusion.21
  94.4 0.7 convert_element_type.152
  95.1 1.0 copy.39
  96.3 1.3 %fusion.4 = bf16[2,32,1152]{2,1,0:T(8,128)(2,1)S(1)} fusion(bf16[2,32,576]{2,1,0:T(8,128)(2,1)S(1)} %convert_element_type.156, bf16[576,1152]{1,0:T(8,128)(2,1)S(1)} %copy-done.2, f32[2,1,2,32,1152]{4,3,2,1,0:T(8,128)} %copy-done.5, f32[1152]{0:T(1024)} %get-tuple-element.3), kind=kOutput, calls=%fused_computation.9 | convolution fusion | flops 85155840 | bytes 1847808 | tf_op jit(solution)/shard_map/dot_general | solution.py:86
  97.7 0.4 convolution_convert_fusion.1
  98.2 0.3 copy-done.7
  98.5 0.2 fusion.76
  99.0 0.3 fusion.23
  99.5 0.2 fusion.75
  100.0 0.3 fusion.25
  100.4 7.9 %all-gather.12.cloned.1.call-done = bf16[576,1152]{1,0:T(8,128)(2,1)} async-done(((bf16[144,1152]{1,0:T(8,128)(2,1)}), bf16[576,1152]{1,0:T(8,128)(2,1)}) %all-gather.12.cloned.1.call-update) | async-done | bytes 1327120 | tf_op jit(solution)/shard_map/all_gather | solution.py:65
  108.3 1.8 %fusion.7 = bf16[1,1,2,32,1152]{4,3,2,1,0:T(8,128)(2,1)S(1)} fusion(bf16[576,1152]{1,0:T(8,128)(2,1)} %all-gather.12.cloned.1.call-done, bf16[2,32,1152]{2,1,0:T(8,128)(2,1)S(1)} %fusion.2, bf16[1,1,32,576]{3,2,1,0:T(8,128)(2,1)S(1)} %copy-done.11, bf16[1,1,32,576]{3,2,1,0:T(8,128)(2,1)S(1)} %convert_element_type.149), kind=kOutput, calls=%fused_computation.12 | convolution fusion | flops 85192704 | bytes 1695744 | tf_op jit(solution)/shard_map/dot_general | solution.py:99
  110.2 0.4 fusion.6
  110.5 0.7 pad_maximum_fusion
  (76 shorter events, 3.7 us)
Async XLA Ops:
  7.2 2.8 %copy-start = (f32[20,3,1152]{2,0,1:T(8,128)S(1)}, f32[20,3,1152]{2,0,1:T(8,128)}, u32[]{:S(2)}) copy-start(f32[20,3,1152]{2,0,1:T(8,128)} %param.17) | copy-start | bytes 829444
  7.2 2.8 %copy-start.18 = (s32[1,2]{1,0:T(1,128)S(1)}, s32[1,2]{1,0:T(1,128)}, u32[]{:S(2)}) copy-start(s32[1,2]{1,0:T(1,128)} %param.16) | copy-start | bytes 28
  7.2 3.8 %copy-start.4 = (bf16[2,1,2,32,1152]{4,3,2,1,0:T(8,128)(2,1)S(1)}, bf16[2,1,2,32,1152]{4,3,2,1,0:T(8,128)(2,1)}, u32[]{:S(2)}) copy-start(bf16[2,1,2,32,1152]{4,3,2,1,0:T(8,128)(2,1)} %param.11) | copy-start | bytes 884740
  7.2 40.8 %all-gather.6.cloned.1.call-start = ((), (), s32[]{:S(2)}) async-start(), calls=%async_computation | async-start | bytes 5160960 | tf_op jit(solution)/shard_map/all_gather | solution.py:60
  7.9 65.9 %all-gather.8.cloned.1.call-start = ((), (), s32[]{:S(2)}) async-start(), calls=%async_computation.1 | async-start | bytes 1658880 | tf_op jit(solution)/shard_map/all_gather | solution.py:63
  8.7 2.7 %copy-start.16 = (bf16[1,2,32,1152]{3,2,1,0:T(8,128)(2,1)S(1)}, bf16[1,2,32,1152]{3,2,1,0:T(8,128)(2,1)}, u32[]{:S(2)}) copy-start(bf16[1,2,32,1152]{3,2,1,0:T(8,128)(2,1)} %param.12) | copy-start | bytes 442372
  8.7 79.9 %all-gather.10.cloned.1.call-start = ((), (), s32[]{:S(2)}) async-start(), calls=%async_computation.2 | async-start | bytes 1843200 | tf_op jit(solution)/shard_map/all_gather | solution.py:64
  9.4 98.9 %all-gather.12.cloned.1.call-start = ((), (), s32[]{:S(2)}) async-start(), calls=%async_computation.3 | async-start | bytes 1658880 | tf_op jit(solution)/shard_map/all_gather | solution.py:65
  10.0 19.6 %copy-start.10 = (bf16[1,128,1152]{2,1,0:T(8,128)(2,1)S(1)}, bf16[1,128,1152]{2,1,0:T(8,128)(2,1)}, u32[]{:S(2)}) copy-start(bf16[1,128,1152]{2,1,0:T(8,128)(2,1)} %param.13) | copy-start | bytes 884740
  11.1 62.7 %copy-start.5 = (f32[2,1,2,32,1152]{4,3,2,1,0:T(8,128)}, f32[2,1,2,32,1152]{4,3,2,1,0:T(8,128)S(1)}, u32[]{:S(2)}) copy-start(f32[2,1,2,32,1152]{4,3,2,1,0:T(8,128)S(1)} %convert_element_type.138) | copy-start | bytes 1769476
  11.1 20.2 %copy-start.17 = (bf16[32,1152]{1,0:T(8,128)(2,1)S(1)}, bf16[32,1152]{1,0:T(8,128)(2,1)}, u32[]{:S(2)}) copy-start(bf16[32,1152]{1,0:T(8,128)(2,1)} %param.14) | copy-start | bytes 221188
  29.8 61.4 %copy-start.6 = (bf16[1,128,576]{1,2,0:T(8,128)(2,1)}, bf16[1,128,576]{1,2,0:T(8,128)(2,1)S(1)}, u32[]{:S(2)}) copy-start(bf16[1,128,576]{1,2,0:T(8,128)(2,1)S(1)} %copy.28) | copy-start | bytes 442372
  39.5 52.4 %copy-start.8 = (bf16[1,128,576]{1,2,0:T(8,128)(2,1)}, bf16[1,128,576]{1,2,0:T(8,128)(2,1)S(1)}, u32[]{:S(2)}) copy-start(bf16[1,128,576]{1,2,0:T(8,128)(2,1)S(1)} %copy.32) | copy-start | bytes 442372
  90.4 1.3 %copy-start.14 = (bf16[1,128,576]{1,2,0:T(8,128)(2,1)S(1)}, bf16[1,128,576]{1,2,0:T(8,128)(2,1)}, u32[]{:S(2)}) copy-start(bf16[1,128,576]{1,2,0:T(8,128)(2,1)} %copy.30) | copy-start | bytes 442372
  92.2 1.8 %copy-start.12 = (bf16[1,128,576]{1,2,0:T(8,128)(2,1)S(1)}, bf16[1,128,576]{1,2,0:T(8,128)(2,1)}, u32[]{:S(2)}) copy-start(bf16[1,128,576]{1,2,0:T(8,128)(2,1)} %copy.34) | copy-start | bytes 442372
  93.0 3.3 %copy-start.2 = (bf16[576,1152]{1,0:T(8,128)(2,1)S(1)}, bf16[576,1152]{1,0:T(8,128)(2,1)}, u32[]{:S(2)}) copy-start(bf16[576,1152]{1,0:T(8,128)(2,1)} %all-gather.8.cloned.1.call-done) | copy-start | bytes 3981316
  94.3 3.4 %copy-start.1 = (bf16[1152,576]{1,0:T(8,128)(2,1)S(1)}, bf16[1152,576]{1,0:T(8,128)(2,1)}, u32[]{:S(2)}) copy-start(bf16[1152,576]{1,0:T(8,128)(2,1)} %all-gather.10.cloned.1.call-done) | copy-start | bytes 3981316
  97.6 0.9 copy-start.7
  97.6 1.4 %copy-start.15 = (bf16[1,128,576]{1,2,0:T(8,128)(2,1)S(1)}, bf16[1,128,576]{1,2,0:T(8,128)(2,1)}, u32[]{:S(2)}) copy-start(bf16[1,128,576]{1,2,0:T(8,128)(2,1)} %copy.30) | copy-start | bytes 442372
  97.6 1.9 %copy-start.9 = (bf16[1,128,576]{1,2,0:T(8,128)(2,1)S(1)}, bf16[1,128,576]{1,2,0:T(8,128)(2,1)}, u32[]{:S(2)}) copy-start(bf16[1,128,576]{1,2,0:T(8,128)(2,1)} %copy-done.8) | copy-start | bytes 442372
  98.0 1.9 %copy-start.13 = (bf16[1,128,576]{1,2,0:T(8,128)(2,1)S(1)}, bf16[1,128,576]{1,2,0:T(8,128)(2,1)}, u32[]{:S(2)}) copy-start(bf16[1,128,576]{1,2,0:T(8,128)(2,1)} %copy.34) | copy-start | bytes 442372
  98.8 9.6 %copy-start.11 = (bf16[1,1,32,576]{3,2,1,0:T(8,128)(2,1)S(1)}, bf16[1,1,32,576]{3,2,1,0:T(8,128)(2,1)}, u32[]{:S(2)}) copy-start(bf16[1,1,32,576]{3,2,1,0:T(8,128)(2,1)} %convert_element_type.152) | copy-start | bytes 110596
  108.3 1.8 %copy-start.3 = (bf16[576,1152]{1,0:T(8,128)(2,1)S(1)}, bf16[576,1152]{1,0:T(8,128)(2,1)}, u32[]{:S(2)}) copy-start(bf16[576,1152]{1,0:T(8,128)(2,1)} %all-gather.12.cloned.1.call-done) | copy-start | bytes 3981316
Sparse Core Ops, SparseCore 0:
  9.6 38.3 all-gather.5
  49.6 18.2 all-gather.7
  69.5 19.0 all-gather.9
  90.0 18.2 all-gather.11
where the time goes:
time: 118 us
  blocking collectives  43.3 us (37%)
  waiting for transfers between devices  31.1 us (26%)
  matrix products  15.3 us (13%)
  between operations  15 us (13%)
  local copies, waits for them, and re-layouts  10.4 us (9%)
  other arithmetic  2.68 us (2%)
    all_gather x2, blocking collectives, neighbours(): return lax.all_gather(local, 'patch', axis=2, tiled=True)  35.3 us
    all_gather x1, waiting for transfers between devices, per_device(): lax.all_gather(w_cq, 'req', axis=0, tiled=True)  13.1 us
    all_gather x1, waiting for transfers between devices, per_device(): lax.all_gather(w_co, 'req', axis=0, tiled=True)  7.94 us
    all_gather x1, blocking collectives, per_device(): negative = lax.all_gather(uncond_kv, 'req', axis=0, tiled=True)  7.94 us
    all_gather x1, waiting for transfers between devices, per_device(): lax.all_gather(w_qkv, 'req', axis=0, tiled=True)  7.45 us
    dot_general x1, matrix products, per_device(): jnp.dot(flat, lax.all_gather(w_qkv, 'req', axis=0, tiled=True), preferred...  3.82 us
    dot_general x2, matrix products, per_device(): jnp.dot(attended.reshape(-1, inner), whole_out, preferred_element_type=jn...  3.04 us
    unnamed x4, waiting for transfers between devices  2.58 us
  transfers between devices with their start and end apart: 4, of which 3 were waited for; matrix products, arithmetic and copies ran while one was open for 21% of the time, Pallas kernels for 0%

commit v1 on v0

v1 whole, which is shorter than its diff:
```python
import functools
import math

import jax
import jax.numpy as jnp
from jax import lax
from jax.experimental import pallas as pl
from jax.experimental.pallas import tpu as pltpu
from jax.sharding import PartitionSpec as P

HEADS = 8
HDIM = 72
CORES = 2
LANES = 128
MESH = pl.DeviceIdType.MESH

QKV, OUT, CQ, CO, NEG = range(5)


def spread(which, start, stop, groups):
    width = (stop - start) // (LANES * groups) * LANES
    chunks = []
    if width:
        chunks.append((which, start, width, True))
    if stop > start + groups * width:
        chunks.append((which, start + groups * width, stop - start - groups * width, False))
    return chunks


def plan(inner, width, groups):
    low = inner // LANES * LANES
    first = spread(QKV, low, 3 * inner, groups)
    stages = [
        first,
        spread(QKV, 0, low, groups),
        spread(OUT, 0, width, groups),
        spread(CQ, 0, inner, groups) + spread(NEG, 0, 2 * inner, groups),
        spread(CO, 0, width, groups),
    ]
    return stages


def times(left, w_ref):
    n, rows, _ = w_ref.shape
    if rows % 16 == 0:
        return jnp.dot(
            left,
            w_ref[...].reshape(n * rows, w_ref.shape[2]),
            preferred_element_type=jnp.float32,
        )
    total = None
    for s in range(n):
        term = jnp.dot(
            left[:, s * rows : (s + 1) * rows], w_ref[s], preferred_element_type=jnp.float32
        )
        total = term if total is None else total + term
    return total


def head_mask(lanes, offset, dtype):
    lane = lax.broadcasted_iota(jnp.int32, (HEADS, 1, lanes), 2) - offset
    first = lax.broadcasted_iota(jnp.int32, (HEADS, 1, lanes), 0) * HDIM
    return jnp.where((lane >= first) & (lane < first + HDIM), 1.0, 0.0).astype(dtype)


def attend(query, keys, values, q_mask, v_mask, count):
    rows, inner = query.shape
    stacked = (query[None] * q_mask).reshape(HEADS * rows, inner)
    scores = lax.dot_general(
        stacked, keys, (((1,), (1,)), ((), ())), preferred_element_type=jnp.float32
    ) * (1.0 / math.sqrt(HDIM))
    if count is not None:
        place = lax.broadcasted_iota(jnp.int32, scores.shape, 1)
        scores = jnp.where(place < count, scores, -1e30)
    expo = jnp.exp(scores - jnp.max(scores, axis=-1, keepdims=True))
    total = jnp.sum(expo, axis=-1, keepdims=True)
    summed = jnp.dot(expo.astype(jnp.bfloat16), values, preferred_element_type=jnp.float32)
    scaled = (summed * (1.0 / total)).reshape(HEADS, rows, values.shape[1])
    return jnp.sum(scaled * v_mask, axis=0)


def kernel(
    groups, patch_n, req_n, stages,
    len_ref, step_ref, hidden_ref, stale_ref, cond_ref, neg_in, table_ref, qkv_in, out_in, cq_in, co_in,
    mixed_ref, next_ref,
    w_qkv, w_out, w_cq, w_co, w_neg, kv0, kv1, mod_s, query_s, att_s,
    local_sem, own_send, own_recv, x_send, x_recv, y_send, y_recv, fx_send, fx_recv, fy_send, fy_recv,
    s_send, s_recv, f_send, f_recv,
):
    chips = req_n // CORES
    group = lax.axis_index("groups")
    patch = lax.axis_index("patch")
    req = lax.axis_index("req")
    chip, core = req // CORES, req % CORES
    sibling = (group, patch, chip * CORES + (1 - core))
    sources = (qkv_in, out_in, cq_in, co_in, neg_in)
    bufs = (w_qkv, w_out, w_cq, w_co, w_neg)
    inner = cq_in.shape[1]
    low = inner // LANES * LANES
    high = low + LANES if low < inner else low

    def chip_at(delta):
        return lax.rem(chip + (delta + chips), chips) * CORES + core

    def group_at(delta):
        return lax.rem(group + (delta + groups), groups)

    def patch_at(delta):
        return lax.rem(patch + (delta + patch_n), patch_n)

    barrier = pltpu.get_barrier_semaphore()
    friends = [sibling]
    friends += [(group, patch, chip_at(d)) for d in range(1, chips)]
    friends += [(group_at(e), patch, req) for e in range(1, groups)]
    friends += [(group, patch_at(d), req) for d in range(1, patch_n)]
    for friend in friends:
        pl.semaphore_signal(barrier, inc=1, device_id=friend, device_id_type=MESH)
    pl.semaphore_wait(barrier, len(friends))

    chunks = [chunk for stage in stages for chunk in stage]

    def columns(chunk, owner):
        _, start, width, shared = chunk
        if not shared:
            return pl.ds(start, width)
        return pl.ds(pl.multiple_of(start + owner * width, LANES), width)

    def remote(src, dst, send, recv, target):
        return pltpu.make_async_remote_copy(
            src_ref=src, dst_ref=dst, send_sem=send, recv_sem=recv,
            device_id=target, device_id_type=MESH,
        )

    def x_copy(k, d):
        chunk = chunks[k]
        cols = columns(chunk, group)
        return remote(
            sources[chunk[0]].at[:, cols], bufs[chunk[0]].at[req, :, cols],
            x_send.at[k, d - 1], x_recv.at[k, d - 1], (group, patch, chip_at(d)),
        )

    def arrived(k, d, owner, send, recv, target):
        part = bufs[chunks[k][0]].at[chip_at(-d), :, columns(chunks[k], owner)]
        return remote(part, part, send, recv, target)

    def x_arrival(k, d):
        return arrived(k, d, group, x_send.at[k, d - 1], x_recv.at[k, d - 1], sibling)

    def y_copy(k, d, e):
        return arrived(
            k, d, group, y_send.at[k, d - 1, e - 1], y_recv.at[k, d - 1, e - 1],
            (group_at(e), patch, req),
        )

    def y_arrival(k, d, e):
        return arrived(
            k, d, group_at(-e), y_send.at[k, d - 1, e - 1], y_recv.at[k, d - 1, e - 1], sibling
        )

    def fx_copy(k, d):
        return arrived(k, d, group, fx_send.at[k, d - 1], fx_recv.at[k, d - 1], sibling)

    def fy_copy(k, d, e):
        return arrived(
            k, d, group_at(-e), fy_send.at[k, d - 1, e - 1], fy_recv.at[k, d - 1, e - 1], sibling
        )

    def other_core(k, d, owner, send, recv):
        source = lax.rem(chip + (chips - d), chips) * CORES + (1 - core)
        part = bufs[chunks[k][0]].at[source, :, columns(chunks[k], owner)]
        return remote(part, part, send, recv, sibling)

    def own_copy(i, slot):
        return remote(
            sources[i], bufs[i].at[slot], own_send.at[i], own_recv.at[i], sibling
        )

    def keep(i):
        return pltpu.make_async_copy(sources[i], bufs[i].at[req], local_sem.at[i])

    def stale_copy(d, slot):
        return remote(
            stale_ref, kv0.at[slot], s_send.at[d - 1], s_recv.at[d - 1],
            (group, patch_at(d), req),
        )

    def fresh_copy(d, slot):
        return remote(
            kv0.at[patch], kv1.at[slot], f_send.at[d - 1], f_recv.at[d - 1],
            (group, patch_at(d), req),
        )

    index = {}
    place = 0
    for number, stage in enumerate(stages):
        index[number] = list(range(place, place + len(stage)))
        place += len(stage)

    for k in range(len(chunks)):
        for d in range(1, chips):
            x_copy(k, d).start()
    for i in range(len(sources)):
        keep(i).start()
        own_copy(i, req).start()
    for d in range(1, patch_n):
        stale_copy(d, patch).start()

    def relay(number):
        for k in index[number]:
            for d in range(1, chips):
                x_arrival(k, d).wait_recv()
                if chunks[k][3]:
                    for e in range(1, groups):
                        y_copy(k, d, e).start()
                fx_copy(k, d).start()

    def relay_two(number):
        for k in index[number]:
            if chunks[k][3]:
                for d in range(1, chips):
                    for e in range(1, groups):
                        y_arrival(k, d, e).wait_recv()
                        fy_copy(k, d, e).start()

    def land(number):
        for k in index[number]:
            for d in range(1, chips):
                other_core(k, d, group, fx_send.at[k, d - 1], fx_recv.at[k, d - 1]).wait_recv()
                if chunks[k][3]:
                    for e in range(1, groups):
                        other_core(
                            k, d, group_at(-e),
                            fy_send.at[k, d - 1, e - 1], fy_recv.at[k, d - 1, e - 1],
                        ).wait_recv()

    def own_land(i):
        keep(i).wait()
        own_copy(i, chip * CORES + (1 - core)).wait_recv()

    rows = hidden_ref.shape[0] // 2
    images = 2
    tok = rows // images
    width = hidden_ref.shape[1]
    mods = [table_ref[step_ref[0, s]] for s in range(2)]
    for s in range(2):
        source = hidden_ref[s * rows : (s + 1) * rows, :].astype(jnp.float32)
        center = source - jnp.mean(source, axis=-1, keepdims=True)
        spread_ = jnp.mean(center * center, axis=-1, keepdims=True)
        normed = center * lax.rsqrt(spread_ + 1e-06)
        mod_s[s * rows : (s + 1) * rows, :] = (
            normed * (1.0 + mods[s][1:2]) + mods[s][0:1]
        ).astype(jnp.bfloat16)

    def project(first, last, start, stop):
        n, depth, _ = w_qkv.shape
        return jnp.dot(
            mod_s[first:last, :], w_qkv[:, :, start:stop].reshape(n * depth, stop - start),
            preferred_element_type=jnp.float32,
        ).astype(jnp.bfloat16)

    relay(0)
    relay_two(0)
    own_land(QKV)
    land(0)
    fresh0 = project(0, rows, low, 3 * inner)[:, inner - low :]
    kv0[patch] = fresh0.reshape(images, tok, 2 * inner)
    for d in range(1, patch_n):
        fresh_copy(d, patch).start()
    relay(1)
    fresh1 = project(rows, 2 * rows, low, 3 * inner)[:, inner - low :]
    kv1[patch] = fresh1.reshape(images, tok, 2 * inner)
    next_ref[...] = fresh1
    relay_two(1)
    land(1)
    query_s[...] = project(0, 2 * rows, 0, high)[:, :inner]
    relay(2)

    q_mask = head_mask(inner, 0, jnp.bfloat16)
    v_mask = head_mask(2 * inner - low, inner - low, jnp.float32)

    def self_attend(step, buf):
        for image in range(images):
            first = step * rows + image * tok
            pairs = buf[:, image].reshape(patch_n * tok, 2 * inner)
            result = attend(
                query_s[first : first + tok, :], pairs[:, :inner], pairs[:, low:],
                q_mask, v_mask, None,
            )
            att_s[first : first + tok, :] = result[:, inner - low :].astype(jnp.bfloat16)

    for d in range(1, patch_n):
        stale_copy(d, patch_at(-d)).wait_recv()
    self_attend(0, kv0)
    relay_two(2)
    relay(3)
    relay_two(3)
    relay(4)
    for d in range(1, patch_n):
        fresh_copy(d, patch_at(-d)).wait_recv()
    self_attend(1, kv1)
    relay_two(4)
    own_land(OUT)
    land(2)
    projected = times(att_s[...], w_out)
    parts = []
    for s in range(2):
        span = slice(s * rows, (s + 1) * rows)
        parts.append(
            (hidden_ref[span, :].astype(jnp.float32) + mods[s][2:3] * projected[span]).astype(
                jnp.bfloat16
            )
        )
    x_one = jnp.concatenate(parts, axis=0)
    own_land(CQ)
    own_land(NEG)
    land(3)
    cross_query = times(x_one, w_cq).astype(jnp.bfloat16)
    count = len_ref[0]
    n_neg, neg_rows, _ = w_neg.shape
    negative = w_neg[...].reshape(n_neg * neg_rows, 2 * inner)
    for image in range(images):
        pairs = cond_ref[...] if image == 0 else negative
        spans = [slice(s * rows + image * tok, s * rows + (image + 1) * tok) for s in range(2)]
        both = jnp.concatenate([cross_query[span] for span in spans], axis=0)
        result = attend(
            both, pairs[:, :inner], pairs[:, low:], q_mask, v_mask, count if image == 0 else None
        )[:, inner - low :].astype(jnp.bfloat16)
        for s in range(2):
            att_s[spans[s], :] = result[s * tok : (s + 1) * tok]
    own_land(CO)
    land(4)
    added = times(att_s[...], w_co)
    mixed_ref[...] = (x_one.astype(jnp.float32) + added).astype(jnp.bfloat16)

    for k in range(len(chunks)):
        for d in range(1, chips):
            x_copy(k, d).wait_send()
            fx_copy(k, d).wait_send()
            if chunks[k][3]:
                for e in range(1, groups):
                    y_copy(k, d, e).wait_send()
                    fy_copy(k, d, e).wait_send()
    for i in range(len(sources)):
        own_copy(i, req).wait_send()
    for d in range(1, patch_n):
        stale_copy(d, patch).wait_send()
        fresh_copy(d, patch).wait_send()


def solution(mesh):
    groups, patch_n, req_n = mesh.shape["groups"], mesh.shape["patch"], mesh.shape["req"]
    chips = req_n // CORES

    def per_device(
        hidden, stale_kv, cond_kv, uncond_kv, text_len, timestep, mod_table, w_qkv, w_out, w_cq, w_co
    ):
        steps_n, req_here, pair_n, tok, width = hidden.shape
        inner = w_cq.shape[1]
        stages = plan(inner, width, groups)
        count = sum(len(stage) for stage in stages)
        total = steps_n * req_here * pair_n * tok
        vmem = pl.BlockSpec(memory_space=pltpu.VMEM)
        anywhere = pl.BlockSpec(memory_space=pl.ANY)
        smem = pl.BlockSpec(memory_space=pltpu.SMEM)
        weights = (w_qkv, w_out, w_cq, w_co, uncond_kv)
        dma = pltpu.SemaphoreType.DMA
        near = (count, max(chips - 1, 1))
        far = near + (max(groups - 1, 1),)
        line = (max(patch_n - 1, 1),)
        mixed, next_kv = pl.pallas_call(
            functools.partial(kernel, groups, patch_n, req_n, stages),
            out_shape=(
                jax.ShapeDtypeStruct((total, width), jnp.bfloat16),
                jax.ShapeDtypeStruct((pair_n * tok, 2 * inner), jnp.bfloat16),
            ),
            in_specs=[
                smem, smem, vmem, anywhere, vmem, anywhere, vmem,
                anywhere, anywhere, anywhere, anywhere,
            ],
            out_specs=(vmem, vmem),
            scratch_shapes=[pltpu.VMEM((req_n,) + w.shape, jnp.bfloat16) for w in weights]
            + [
                pltpu.VMEM((patch_n, pair_n, tok, 2 * inner), jnp.bfloat16),
                pltpu.VMEM((patch_n, pair_n, tok, 2 * inner), jnp.bfloat16),
                pltpu.VMEM((total, width), jnp.bfloat16),
                pltpu.VMEM((total, inner), jnp.bfloat16),
                pltpu.VMEM((total, inner), jnp.bfloat16),
                dma((5,)), dma((5,)), dma((5,)),
                dma(near), dma(near), dma(far), dma(far), dma(near), dma(near), dma(far), dma(far),
                dma(line), dma(line), dma(line), dma(line),
            ],
            compiler_params=pltpu.CompilerParams(
                collective_id=0, has_side_effects=True, vmem_limit_bytes=48 * 1024 * 1024
            ),
        )(
            text_len, timestep, hidden.reshape(total, width),
            stale_kv.reshape(pair_n, tok, 2 * inner), cond_kv.reshape(cond_kv.shape[1:]),
            uncond_kv, mod_table, w_qkv, w_out, w_cq, w_co,
        )
        return mixed.reshape(hidden.shape), next_kv.reshape(stale_kv.shape)

    placed = (
        P(None, ("groups", "req"), None, "patch", None),
        P(("groups", "req"), None, "patch", None),
        P(("groups", "req"), None, None),
        P("req", None),
        P(("groups", "req")),
        P(("groups", "req"), None),
        P(),
        P("req", None),
        P("req", None),
        P("req", None),
        P("req", None),
    )
    return jax.shard_map(
        per_device,
        mesh=mesh,
        in_specs=placed,
        out_specs=(
            P(None, ("groups", "req"), None, "patch", None),
            P(("groups", "req"), None, "patch", None),
        ),
        check_vma=False,
    )
```

time: 118 us -> 56.8 us (0.48)
  Pallas kernels: 0 us -> 46.7 us
  blocking collectives: 43.3 us -> 0 us
  waiting for transfers between devices: 31.1 us -> 0 us
  matrix products: 15.3 us -> 0 us
  between operations: 15 us -> 1.4 us
  other arithmetic: 2.68 us -> 0 us
  local copies, waits for them, and re-layouts: 10.4 us -> 8.41 us
    pallas_call x0 -> x1, Pallas kernels: none -> 46.7 us  [per_device(): pl.pallas_call(functools.partial(kernel, groups, patch_n, req_n, stages),...]
    all_gather x3 -> x0, blocking collectives: 43.3 us -> none  [the longest x2 35.3 us: neighbours(): return lax.all_gather(local, 'patch', axis=2, tiled=True)]
    all_gather x4 -> x0, waiting for transfers between devices: 28.5 us -> none  [the longest x1 13.1 us: per_device(): lax.all_gather(w_cq, 'req', axis=0, tiled=True)]
    dot_general x20 -> x0, matrix products: 15.3 us -> none  [the longest x1 3.82 us: per_device(): jnp.dot(flat, lax.all_gather(w_qkv, 'req', axis=0, tiled=True), preferred...]
    unnamed x38 -> x21, local copies, waits for them, and re-layouts: 0.44 us -> 8.41 us
    slice x15 -> x0, local copies, waits for them, and re-layouts: 4.63 us -> none  [the longest x4 2.01 us: attend(): v_heads = pairs[:, :, inner:].reshape(batch, keys_n, HEADS, HDIM)]
    convert_element_type x13 -> x0, local copies, waits for them, and re-layouts: 2.71 us -> none  [the longest x12 2.5 us: attend(): return result.reshape(batch, count, inner).astype(jnp.bfloat16)]
    unnamed x4 -> x0, waiting for transfers between devices: 2.58 us -> none
  transfers between devices with their start and end apart: 4 -> 0, of which waited for: 3 -> 0; matrix products, arithmetic and copies ran while one was open for 21% -> 0% of each run, Pallas kernels for 0% -> 0%
where the time goes in v1:
time: 56.8 us; the launch traced here: 56.5 us
  Pallas kernels  46.7 us (82%)
  local copies, waits for them, and re-layouts  8.41 us (15%)
  between operations  1.4 us (2%)
    pallas_call x1, Pallas kernels, per_device(): pl.pallas_call(functools.partial(kernel, groups, patch_n, req_n, stages),...  46.7 us
    unnamed x21, local copies, waits for them, and re-layouts  8.41 us

profile of v1, /device:TPU:0, one launch (start us, length us, event | category | flops | bytes accessed | tf_op | source)
XLA Modules:
  0.0 56.5 jit_solution(12922944588460742236)
XLA Ops:
  0.6 0.0 copy-start.1
  1.3 0.0 copy-start.2
  1.3 0.0 copy-start.8
  1.4 1.1 %copy.13.table_ref = f32[20,3,1152]{2,1,0:T(4,128)S(1)} copy(f32[20,3,1152]{2,0,1:T(8,128)} %param.17) | data formatting | bytes 552960 | tf_op args[6]
  2.5 0.0 copy-done.1
  2.5 0.0 copy-done.2
  2.5 0.0 copy-done.8
  2.5 0.0 copy-start
  2.5 1.2 %copy-done = bf16[288,1728]{1,0:T(8,128)(2,1)S(1)} copy-done((bf16[288,1728]{1,0:T(8,128)(2,1)S(1)}, bf16[288,1728]{1,0:T(8,128)(2,1)}, u32[]{:S(2)}) %copy-start) | copy-done | bytes 995352
  3.7 0.0 copy-start.3
  3.7 1.0 %copy-done.3 = bf16[144,1152]{1,0:T(8,128)(2,1)S(1)} copy-done((bf16[144,1152]{1,0:T(8,128)(2,1)S(1)}, bf16[144,1152]{1,0:T(8,128)(2,1)}, u32[]{:S(2)}) %copy-start.3) | copy-done | bytes 331800
  4.7 0.0 copy-start.4
  4.7 1.0 %copy-done.4 = bf16[2,1,2,32,1152]{4,3,2,1,0:T(8,128)(2,1)S(1)} copy-done((bf16[2,1,2,32,1152]{4,3,2,1,0:T(8,128)(2,1)S(1)}, bf16[2,1,2,32,1152]{4,3,2,1,0:T(8,128)(2,1)}, u32[]{:S(2)}) %copy-start.4) | copy-done | bytes 294936
  5.7 0.0 copy-start.5
  5.7 1.0 %copy-done.5 = bf16[1,128,1152]{2,1,0:T(8,128)(2,1)S(1)} copy-done((bf16[1,128,1152]{2,1,0:T(8,128)(2,1)S(1)}, bf16[1,128,1152]{2,1,0:T(8,128)(2,1)}, u32[]{:S(2)}) %copy-start.5) | copy-done | bytes 294936
  6.6 0.0 copy-start.6
  6.6 0.9 %copy-done.6 = bf16[1,2,32,1152]{3,2,1,0:T(8,128)(2,1)S(1)} copy-done((bf16[1,2,32,1152]{3,2,1,0:T(8,128)(2,1)S(1)}, bf16[1,2,32,1152]{3,2,1,0:T(8,128)(2,1)}, u32[]{:S(2)}) %copy-start.6) | copy-done | bytes 147480
  7.5 0.0 copy-start.7
  7.5 0.9 %copy-done.7 = bf16[32,1152]{1,0:T(8,128)(2,1)S(1)} copy-done((bf16[32,1152]{1,0:T(8,128)(2,1)S(1)}, bf16[32,1152]{1,0:T(8,128)(2,1)}, u32[]{:S(2)}) %copy-start.7) | copy-done | bytes 73752
  8.4 46.7 %shard_map.122 = (bf16[128,1152]{1,0:T(8,128)(2,1)S(1)}, bf16[64,1152]{1,0:T(8,128)(2,1)S(1)}) custom-call(s32[1]{0:T(128)S(6)} %copy.17.len_ref, s32[1,2]{1,0:T(1,128)S(1)} %copy-done.8, bf16[128,1152]{1,0:T(8,128)(2,1)S(1)} %bitcast.7, bf16[2,32,1152]{2,1,0:T(8,128)(2,1)S(1)} %bitcast.10, bf16[128,1152]{1,0:T(8,128)(2,1)S(1)} %bitcast.8, ...), custom_call_target="tpu_custom_call" | custom-call | tf_op jit(solution)/shard_map/pallas_call | solution.py:370
  55.1 0.7 %copy.18 = bf16[2,1,2,32,1152]{4,3,2,1,0:T(8,128)(2,1)} copy(bf16[2,1,2,32,1152]{4,3,2,1,0:T(8,128)(2,1)S(1)} %bitcast.9) | data formatting | bytes 589824
  55.8 0.7 %copy.19 = bf16[1,2,32,1152]{3,2,1,0:T(8,128)(2,1)} copy(bf16[1,2,32,1152]{3,2,1,0:T(8,128)(2,1)S(1)} %bitcast.11) | data formatting | bytes 294912
Async XLA Ops:
  0.6 1.8 %copy-start.1 = (bf16[288,576]{1,0:T(8,128)(2,1)S(1)}, bf16[288,576]{1,0:T(8,128)(2,1)}, u32[]{:S(2)}) copy-start(bf16[288,576]{1,0:T(8,128)(2,1)} %cq_in.1) | copy-start | bytes 995332
  1.3 1.1 %copy-start.2 = (bf16[144,1152]{1,0:T(8,128)(2,1)S(1)}, bf16[144,1152]{1,0:T(8,128)(2,1)}, u32[]{:S(2)}) copy-start(bf16[144,1152]{1,0:T(8,128)(2,1)} %out_in.1) | copy-start | bytes 995332
  1.3 1.1 %copy-start.8 = (s32[1,2]{1,0:T(1,128)S(1)}, s32[1,2]{1,0:T(1,128)}, u32[]{:S(2)}) copy-start(s32[1,2]{1,0:T(1,128)} %step_ref.1) | copy-start | bytes 28
  2.5 1.2 %copy-start = (bf16[288,1728]{1,0:T(8,128)(2,1)S(1)}, bf16[288,1728]{1,0:T(8,128)(2,1)}, u32[]{:S(2)}) copy-start(bf16[288,1728]{1,0:T(8,128)(2,1)} %qkv_in.1) | copy-start | bytes 2985988
  3.7 1.0 %copy-start.3 = (bf16[144,1152]{1,0:T(8,128)(2,1)S(1)}, bf16[144,1152]{1,0:T(8,128)(2,1)}, u32[]{:S(2)}) copy-start(bf16[144,1152]{1,0:T(8,128)(2,1)} %co_in.1) | copy-start | bytes 995332
  4.7 1.0 %copy-start.4 = (bf16[2,1,2,32,1152]{4,3,2,1,0:T(8,128)(2,1)S(1)}, bf16[2,1,2,32,1152]{4,3,2,1,0:T(8,128)(2,1)}, u32[]{:S(2)}) copy-start(bf16[2,1,2,32,1152]{4,3,2,1,0:T(8,128)(2,1)} %param.11) | copy-start | bytes 884740
  5.7 1.0 %copy-start.5 = (bf16[1,128,1152]{2,1,0:T(8,128)(2,1)S(1)}, bf16[1,128,1152]{2,1,0:T(8,128)(2,1)}, u32[]{:S(2)}) copy-start(bf16[1,128,1152]{2,1,0:T(8,128)(2,1)} %param.13) | copy-start | bytes 884740
  6.6 0.9 %copy-start.6 = (bf16[1,2,32,1152]{3,2,1,0:T(8,128)(2,1)S(1)}, bf16[1,2,32,1152]{3,2,1,0:T(8,128)(2,1)}, u32[]{:S(2)}) copy-start(bf16[1,2,32,1152]{3,2,1,0:T(8,128)(2,1)} %param.12) | copy-start | bytes 442372
  7.5 0.9 %copy-start.7 = (bf16[32,1152]{1,0:T(8,128)(2,1)S(1)}, bf16[32,1152]{1,0:T(8,128)(2,1)}, u32[]{:S(2)}) copy-start(bf16[32,1152]{1,0:T(8,128)(2,1)} %neg_in.1) | copy-start | bytes 221188

commit v2 on v1

--- a/solution.py
+++ b/solution.py
@@ -12,6 +12,8 @@
 HDIM = 72
 CORES = 2
 LANES = 128
+PIECE = 256
+AHEAD = 3
 MESH = pl.DeviceIdType.MESH
 
 QKV, OUT, CQ, CO, NEG = range(5)
@@ -20,8 +22,11 @@
 def spread(which, start, stop, groups):
     width = (stop - start) // (LANES * groups) * LANES
     chunks = []
-    if width:
-        chunks.append((which, start, width, True))
+    place = start
+    while place < start + groups * width:
+        piece = min(PIECE, (start + groups * width - place) // groups)
+        chunks.append((which, place, piece, True))
+        place += groups * piece
     if stop > start + groups * width:
         chunks.append((which, start + groups * width, stop - start - groups * width, False))
     return chunks
@@ -81,10 +86,10 @@
 
 def kernel(
     groups, patch_n, req_n, stages,
-    len_ref, step_ref, hidden_ref, stale_ref, cond_ref, neg_in, table_ref, qkv_in, out_in, cq_in, co_in,
+    len_ref, step_ref, hidden_in, stale_ref, cond_in, neg_in, table_in, qkv_in, out_in, cq_in, co_in,
     mixed_ref, next_ref,
     w_qkv, w_out, w_cq, w_co, w_neg, kv0, kv1, mod_s, query_s, att_s,
-    local_sem, own_send, own_recv, x_send, x_recv, y_send, y_recv, fx_send, fx_recv, fy_send, fy_recv,
+    hidden_ref, cond_ref, table_ref, in_sem, local_sem, own_send, own_recv, x_send, x_recv, y_send, y_recv, fx_send, fx_recv, fy_send, fy_recv,
     s_send, s_recv, f_send, f_recv,
 ):
     chips = req_n // CORES
@@ -108,6 +113,14 @@
     def patch_at(delta):
         return lax.rem(patch + (delta + patch_n), patch_n)
 
+    staged = [
+        pltpu.make_async_copy(src, dst, in_sem.at[i])
+        for i, (src, dst) in enumerate(
+            ((hidden_in, hidden_ref), (table_in, table_ref), (cond_in, cond_ref))
+        )
+    ]
+    for copy in staged:
+        copy.start()
     barrier = pltpu.get_barrier_semaphore()
     friends = [sibling]
     friends += [(group, patch, chip_at(d)) for d in range(1, chips)]
@@ -196,7 +209,7 @@
         index[number] = list(range(place, place + len(stage)))
         place += len(stage)
 
-    for k in range(len(chunks)):
+    for k in range(min(AHEAD, len(chunks))):
         for d in range(1, chips):
             x_copy(k, d).start()
     for i in range(len(sources)):
@@ -213,6 +226,8 @@
                     for e in range(1, groups):
                         y_copy(k, d, e).start()
                 fx_copy(k, d).start()
+                if k + AHEAD < len(chunks):
+                    x_copy(k + AHEAD, d).start()
 
     def relay_two(number):
         for k in index[number]:
@@ -241,14 +256,18 @@
     images = 2
     tok = rows // images
     width = hidden_ref.shape[1]
-    mods = [table_ref[step_ref[0, s]] for s in range(2)]
+    staged[0].wait()
+    staged[1].wait()
+    mods = [
+        [table_ref[c, pl.ds(step_ref[0, s], 1), :] for c in range(3)] for s in range(2)
+    ]
     for s in range(2):
         source = hidden_ref[s * rows : (s + 1) * rows, :].astype(jnp.float32)
         center = source - jnp.mean(source, axis=-1, keepdims=True)
         spread_ = jnp.mean(center * center, axis=-1, keepdims=True)
         normed = center * lax.rsqrt(spread_ + 1e-06)
         mod_s[s * rows : (s + 1) * rows, :] = (
-            normed * (1.0 + mods[s][1:2]) + mods[s][0:1]
+            normed * (1.0 + mods[s][1]) + mods[s][0]
         ).astype(jnp.bfloat16)
 
     def project(first, last, start, stop):
@@ -306,13 +325,14 @@
     for s in range(2):
         span = slice(s * rows, (s + 1) * rows)
         parts.append(
-            (hidden_ref[span, :].astype(jnp.float32) + mods[s][2:3] * projected[span]).astype(
+            (hidden_ref[span, :].astype(jnp.float32) + mods[s][2] * projected[span]).astype(
                 jnp.bfloat16
             )
         )
     x_one = jnp.concatenate(parts, axis=0)
     own_land(CQ)
     own_land(NEG)
+    staged[2].wait()
     land(3)
     cross_query = times(x_one, w_cq).astype(jnp.bfloat16)
     count = len_ref[0]
@@ -360,10 +380,11 @@
         count = sum(len(stage) for stage in stages)
         total = steps_n * req_here * pair_n * tok
         vmem = pl.BlockSpec(memory_space=pltpu.VMEM)
-        anywhere = pl.BlockSpec(memory_space=pl.ANY)
+        hbm = pl.BlockSpec(memory_space=pltpu.HBM)
         smem = pl.BlockSpec(memory_space=pltpu.SMEM)
         weights = (w_qkv, w_out, w_cq, w_co, uncond_kv)
         dma = pltpu.SemaphoreType.DMA
+        table = jnp.transpose(mod_table, (1, 0, 2))
         near = (count, max(chips - 1, 1))
         far = near + (max(groups - 1, 1),)
         line = (max(patch_n - 1, 1),)
@@ -374,8 +395,7 @@
                 jax.ShapeDtypeStruct((pair_n * tok, 2 * inner), jnp.bfloat16),
             ),
             in_specs=[
-                smem, smem, vmem, anywhere, vmem, anywhere, vmem,
-                anywhere, anywhere, anywhere, anywhere,
+                smem, smem, hbm, hbm, hbm, hbm, hbm, hbm, hbm, hbm, hbm,
             ],
             out_specs=(vmem, vmem),
             scratch_shapes=[pltpu.VMEM((req_n,) + w.shape, jnp.bfloat16) for w in weights]
@@ -385,7 +405,10 @@
                 pltpu.VMEM((total, width), jnp.bfloat16),
                 pltpu.VMEM((total, inner), jnp.bfloat16),
                 pltpu.VMEM((total, inner), jnp.bfloat16),
-                dma((5,)), dma((5,)), dma((5,)),
+                pltpu.VMEM((total, width), jnp.bfloat16),
+                pltpu.VMEM(cond_kv.shape[1:], jnp.bfloat16),
+                pltpu.VMEM(table.shape, jnp.float32),
+                dma((3,)), dma((5,)), dma((5,)), dma((5,)),
                 dma(near), dma(near), dma(far), dma(far), dma(near), dma(near), dma(far), dma(far),
                 dma(line), dma(line), dma(line), dma(line),
             ],
@@ -393,9 +416,15 @@
                 collective_id=0, has_side_effects=True, vmem_limit_bytes=48 * 1024 * 1024
             ),
         )(
-            text_len, timestep, hidden.reshape(total, width),
-            stale_kv.reshape(pair_n, tok, 2 * inner), cond_kv.reshape(cond_kv.shape[1:]),
-            uncond_kv, mod_table, w_qkv, w_out, w_cq, w_co,
+            text_len, timestep,
+            *(
+                pltpu.with_memory_space_constraint(value, pltpu.HBM)
+                for value in (
+                    hidden.reshape(total, width), stale_kv.reshape(pair_n, tok, 2 * inner),
+                    cond_kv.reshape(cond_kv.shape[1:]), uncond_kv, table,
+                    w_qkv, w_out, w_cq, w_co,
+                )
+            ),
         )
         return mixed.reshape(hidden.shape), next_kv.reshape(stale_kv.shape)
 

time: 56.8 us -> 52.7 us (0.928)
  local copies, waits for them, and re-layouts: 8.41 us -> 2.03 us
  Pallas kernels: 46.7 us -> 49.2 us
    unnamed x21 -> x4, local copies, waits for them, and re-layouts: 8.41 us -> 2.03 us
    pallas_call x1, Pallas kernels: 46.7 us -> 49.2 us  [per_device(): pl.pallas_call(functools.partial(kernel, groups, patch_n, req_n, stages),...]
where the time goes in v2:
time: 52.7 us; the launch traced here: 52.5 us
  Pallas kernels  49.2 us (93%)
  local copies, waits for them, and re-layouts  2.03 us (4%)
  between operations  1.3 us (2%)
    pallas_call x1, Pallas kernels, per_device(): pl.pallas_call(functools.partial(kernel, groups, patch_n, req_n, stages),...  49.2 us
    unnamed x4, local copies, waits for them, and re-layouts  2.03 us

profile of v2, /device:TPU:0, one launch (start us, length us, event | category | flops | bytes accessed | tf_op | source)
XLA Modules:
  0.0 52.5 jit_solution(12233851608011104768)
XLA Ops:
  1.3 0.0 copy-start
  1.3 0.6 %copy-done = s32[1,2]{1,0:T(1,128)S(1)} copy-done((s32[1,2]{1,0:T(1,128)S(1)}, s32[1,2]{1,0:T(1,128)}, u32[]{:S(2)}) %copy-start) | copy-done | bytes 32
  1.9 49.2 %shard_map.122 = (bf16[128,1152]{1,0:T(8,128)(2,1)S(1)}, bf16[64,1152]{1,0:T(8,128)(2,1)S(1)}) custom-call(s32[1]{0:T(128)S(6)} %copy.16.len_ref, s32[1,2]{1,0:T(1,128)S(1)} %copy-done, bf16[128,1152]{1,0:T(8,128)(2,1)} %bitcast.11, bf16[2,32,1152]{2,1,0:T(8,128)(2,1)} %bitcast.13, bf16[128,1152]{1,0:T(8,128)(2,1)} %bitcast.12, bf16[32,1152]{1,0:T(8,128)(2,1)} %neg_in.1, ...), custom_call_target="tpu_custom_call" | custom-call | tf_op jit(solution)/shard_map/pallas_call | solution.py:391
  51.1 0.7 %copy.17 = bf16[2,1,2,32,1152]{4,3,2,1,0:T(8,128)(2,1)} copy(bf16[2,1,2,32,1152]{4,3,2,1,0:T(8,128)(2,1)S(1)} %bitcast.8) | data formatting | bytes 589824
  51.9 0.7 %copy.18 = bf16[1,2,32,1152]{3,2,1,0:T(8,128)(2,1)} copy(bf16[1,2,32,1152]{3,2,1,0:T(8,128)(2,1)S(1)} %bitcast.9) | data formatting | bytes 294912
Async XLA Ops:
  1.3 0.7 %copy-start = (s32[1,2]{1,0:T(1,128)S(1)}, s32[1,2]{1,0:T(1,128)}, u32[]{:S(2)}) copy-start(s32[1,2]{1,0:T(1,128)} %step_ref.1) | copy-start | bytes 28

commit v3 on v2

--- a/solution.py
+++ b/solution.py
@@ -13,7 +13,7 @@
 CORES = 2
 LANES = 128
 PIECE = 256
-AHEAD = 3
+AHEAD = 6
 MESH = pl.DeviceIdType.MESH
 
 QKV, OUT, CQ, CO, NEG = range(5)

time: 52.7 us -> 51.7 us (0.981)
  Pallas kernels: 49.2 us -> 48.2 us
    pallas_call x1, Pallas kernels: 49.2 us -> 48.2 us  [per_device(): pl.pallas_call(functools.partial(kernel, groups, patch_n, req_n, stages),...]
where the time goes in v3:
time: 51.7 us; the launch traced here: 51.5 us
  Pallas kernels  48.2 us (93%)
  local copies, waits for them, and re-layouts  2.03 us (4%)
  between operations  1.3 us (3%)
    pallas_call x1, Pallas kernels, per_device(): pl.pallas_call(functools.partial(kernel, groups, patch_n, req_n, stages),...  48.2 us
    unnamed x4, local copies, waits for them, and re-layouts  2.03 us

profile of v3, /device:TPU:0, one launch (start us, length us, event | category | flops | bytes accessed | tf_op | source)
XLA Modules:
  0.0 51.5 jit_solution(5219163443058505151)
XLA Ops:
  1.3 0.0 copy-start
  1.3 0.6 %copy-done = s32[1,2]{1,0:T(1,128)S(1)} copy-done((s32[1,2]{1,0:T(1,128)S(1)}, s32[1,2]{1,0:T(1,128)}, u32[]{:S(2)}) %copy-start) | copy-done | bytes 32
  1.9 48.2 %shard_map.122 = (bf16[128,1152]{1,0:T(8,128)(2,1)S(1)}, bf16[64,1152]{1,0:T(8,128)(2,1)S(1)}) custom-call(s32[1]{0:T(128)S(6)} %copy.16.len_ref, s32[1,2]{1,0:T(1,128)S(1)} %copy-done, bf16[128,1152]{1,0:T(8,128)(2,1)} %bitcast.11, bf16[2,32,1152]{2,1,0:T(8,128)(2,1)} %bitcast.13, bf16[128,1152]{1,0:T(8,128)(2,1)} %bitcast.12, bf16[32,1152]{1,0:T(8,128)(2,1)} %neg_in.1, ...), custom_call_target="tpu_custom_call" | custom-call | tf_op jit(solution)/shard_map/pallas_call | solution.py:391
  50.2 0.7 %copy.17 = bf16[2,1,2,32,1152]{4,3,2,1,0:T(8,128)(2,1)} copy(bf16[2,1,2,32,1152]{4,3,2,1,0:T(8,128)(2,1)S(1)} %bitcast.8) | data formatting | bytes 589824
  50.9 0.7 %copy.18 = bf16[1,2,32,1152]{3,2,1,0:T(8,128)(2,1)} copy(bf16[1,2,32,1152]{3,2,1,0:T(8,128)(2,1)S(1)} %bitcast.9) | data formatting | bytes 294912
Async XLA Ops:
  1.3 0.7 %copy-start = (s32[1,2]{1,0:T(1,128)S(1)}, s32[1,2]{1,0:T(1,128)}, u32[]{:S(2)}) copy-start(s32[1,2]{1,0:T(1,128)} %step_ref.1) | copy-start | bytes 28
